TPU v7x, 128 devices: a whole 4x4x4 slice. The times are simulated.
128 devices in a mesh: gx: 8 (over y, x_lo), gy: 8 (over z, core), sa: 2 (over x_hi).
Axes of the slice: x: 4 (x_hi: 2, x_lo: 2; x = x_hi * 2 + x_lo), y: 4, z: 4, core: 2. Of those that a mesh axis runs over, the one named last changes fastest.
Arguments:
- sweep_bricks: bfloat16 [8, 8, 256, 64, 128], P('gx', 'gy', 'sa'), may hold values from -24 to 24
- target_rank: int32 [8, 8, 256, 1], P('gx', 'gy', 'sa'), may hold values from 0 to 15; in each aligned block of 128 rows (0 to 127, 128 to 255, ..., all dimensions but the last counted through in order) at most 16 rows name the same one
- target_slot: int32 [8, 8, 256], P('gx', 'gy', 'sa'), may hold values from 0 to 15
- conv_first: bfloat16 [27, 128, 128], replicated, may hold values from -0.109375 to 0.109375
- conv_second: bfloat16 [27, 128, 128], replicated, may hold values from -0.109375 to 0.109375
- norm_gain: float32 [128], replicated, may hold values from 0.1 to 1.9
- out_grad: bfloat16 [64, 128, 16, 128], P('gx', 'gy', 'sa'), may hold values from -6 to 6
Outputs:
- block_out: bfloat16 [64, 128, 16, 128], P('gx', 'gy', 'sa')
- grid_grad: bfloat16 [64, 128, 16, 128], P('gx', 'gy', 'sa')
- conv_first_grad: float32 [27, 128, 128], replicated
- conv_second_grad: float32 [27, 128, 128], replicated
- gain_grad: float32 [128], replicated
Inputs may be any that keep to these rules, and one draw needn't show every extreme that they name: `target_rank`: A contribution stays at its gy index; at most 16 of the rows of one device name the same destination, and some destination receives exactly 16 of them. `target_slot`: brick position (bx * 4 + by) * 2 + bz of the destination's 2 x 4 x 2 bricks.
All inputs are finite; a program needn't handle non-finite values.
Results may differ from a plain program's by a relative error of at most 0.017.
Values may be sent and summed in bfloat16 or wider, within the bound.
No kernel may reach another device: no remote copies, remote signals or barrier semaphores. Data moves between devices by JAX's collectives and lax.ppermute only.
A program may use at most 64 MiB of HBM per device.

v0:
```python
import math
import jax
import jax.numpy as jnp
from jax import lax
from jax.sharding import PartitionSpec as P

BX = 2
BY = 4
BZ = 2
epsilon = 1e-06


def extended(block, sides, width):
    for axis, dim in sides:
        count = lax.axis_size(axis)
        forward = [(i, i + 1) for i in range(count - 1)]
        backward = [(target, source) for source, target in forward]
        low = lax.ppermute(
            lax.slice_in_dim(block, block.shape[dim] - width, None, axis=dim), axis, forward
        )
        high = lax.ppermute(lax.slice_in_dim(block, 0, width, axis=dim), axis, backward)
        block = jnp.concatenate([low, block, high], axis=dim)
    return block


def surround(volume):
    return extended(volume, (("gx", 0), ("gy", 1), ("sa", 2)), 1)


def apply_conv(padded, weights):
    extent_x = padded.shape[0] - 2
    extent_y = padded.shape[1] - 2
    extent_z = padded.shape[2] - 2
    channels = padded.shape[3]
    summed = jnp.zeros((extent_x * extent_y * extent_z, weights.shape[2]), jnp.float32)
    for offset in range(27):
        along_x, along_y, along_z = (offset // 9, offset // 3 % 3, offset % 3)
        window = padded[
            along_x : along_x + extent_x, along_y : along_y + extent_y, along_z : along_z + extent_z
        ]
        summed = summed + jnp.dot(
            window.reshape(-1, channels), weights[offset], preferred_element_type=jnp.float32
        )
    return summed.reshape(extent_x, extent_y, extent_z, weights.shape[2])


def transposed_conv(padded, weights):
    extent_x = padded.shape[0] - 2
    extent_y = padded.shape[1] - 2
    extent_z = padded.shape[2] - 2
    channels = padded.shape[3]
    summed = jnp.zeros((extent_x * extent_y * extent_z, weights.shape[1]), jnp.float32)
    for offset in range(27):
        along_x, along_y, along_z = (2 - offset // 9, 2 - offset // 3 % 3, 2 - offset % 3)
        window = padded[
            along_x : along_x + extent_x, along_y : along_y + extent_y, along_z : along_z + extent_z
        ]
        summed = summed + lax.dot_general(
            window.reshape(-1, channels),
            weights[offset],
            (((1,), (1,)), ((), ())),
            preferred_element_type=jnp.float32,
        )
    return summed.reshape(extent_x, extent_y, extent_z, weights.shape[1])


def weight_grads(padded, grads):
    extent_x, extent_y, extent_z, channels = grads.shape
    grad_rows = grads.reshape(-1, channels)
    pieces = []
    for offset in range(27):
        along_x, along_y, along_z = (offset // 9, offset // 3 % 3, offset % 3)
        window = padded[
            along_x : along_x + extent_x, along_y : along_y + extent_y, along_z : along_z + extent_z
        ]
        pieces.append(
            lax.dot_general(
                window.reshape(-1, padded.shape[3]),
                grad_rows,
                (((0,), (0,)), ((), ())),
                preferred_element_type=jnp.float32,
            )
        )
    return jnp.stack(pieces)


def to_voxels(values):
    moved = values.transpose(0, 3, 1, 4, 2, 5, 6)
    return moved.reshape(BX * 4, BY * 4, BZ * 4, values.shape[6])


def local(sweep_bricks, target_rank, target_slot, conv_first, conv_second, norm_gain, out_grad):
    groups = lax.axis_size("gx") * lax.axis_size("sa")
    sends = sweep_bricks.shape[2]
    channels = sweep_bricks.shape[4]
    capacity = 2 * sends // groups
    positions = BX * BY * BZ
    ranks = target_rank.reshape(sends)
    slot_ids = target_slot.reshape(sends)
    member = (ranks[:, None] == jnp.arange(groups, dtype=jnp.int32)[None, :]).astype(jnp.int32)
    earlier = jnp.sum((jnp.cumsum(member, axis=0) - member) * member, axis=1)
    places = ranks * capacity + earlier
    placing = places[None, :] == jnp.arange(groups * capacity, dtype=jnp.int32)[:, None]
    rows = sweep_bricks.reshape(sends, -1)
    outgoing = jnp.dot(
        placing.astype(jnp.bfloat16), rows, preferred_element_type=jnp.float32
    ).astype(jnp.bfloat16)
    labels = (
        (jnp.sum(jnp.where(placing, slot_ids[None, :] + 1, 0), axis=1) - 1)
        .astype(jnp.float32)
        .astype(jnp.bfloat16)
    )
    arrived, arrived_labels = (
        lax.all_to_all(outgoing, ("gx", "sa"), split_axis=0, concat_axis=0, tiled=True),
        lax.all_to_all(labels, ("gx", "sa"), split_axis=0, concat_axis=0, tiled=True),
    )
    choose = (
        arrived_labels.astype(jnp.float32)[None, :]
        == jnp.arange(positions, dtype=jnp.float32)[:, None]
    )
    brick_sums = jnp.dot(choose.astype(jnp.bfloat16), arrived, preferred_element_type=jnp.float32)
    grid = to_voxels(brick_sums.astype(jnp.bfloat16).reshape(BX, BY, BZ, 4, 4, 4, channels))
    filled = jnp.any(choose, axis=1).astype(jnp.float32).reshape(BX, BY, BZ, 1, 1, 1, 1)
    live = to_voxels(jnp.broadcast_to(filled, (BX, BY, BZ, 4, 4, 4, 1)))
    grid_f = grid.astype(jnp.float32)
    inverse = lax.rsqrt(jnp.mean(grid_f * grid_f, axis=-1, keepdims=True) + epsilon)
    normed = (grid_f * inverse * norm_gain).astype(jnp.bfloat16)
    normed_pad = surround(normed)
    before_act = live * apply_conv(normed_pad, conv_first)
    sigmoid_act = jax.nn.sigmoid(before_act)
    active = (before_act * sigmoid_act).astype(jnp.bfloat16)
    active_pad = surround(active)
    branch = live * apply_conv(active_pad, conv_second)
    block_out = (grid_f + branch).astype(jnp.bfloat16)
    out_grad_f = out_grad.astype(jnp.float32)
    out_masked = (live * out_grad_f).astype(jnp.bfloat16)
    masked_pad = surround(out_masked)
    second_grad = weight_grads(active_pad, out_masked)
    active_grad = transposed_conv(masked_pad, conv_second)
    pre_grad = (active_grad * sigmoid_act * (1.0 + before_act * (1.0 - sigmoid_act))).astype(
        jnp.bfloat16
    )
    pre_pad = surround(pre_grad)
    first_grad = weight_grads(normed_pad, pre_grad)
    normed_grad = live * transposed_conv(pre_pad, conv_first)
    gain_grad = jnp.sum((normed_grad * grid_f * inverse).reshape(-1, channels), axis=0)
    first_total, second_total, gain_total = lax.psum(
        (first_grad, second_grad, gain_grad), ("gx", "gy", "sa")
    )
    upstream = normed_grad * norm_gain
    centred = jnp.mean(grid_f * upstream, axis=-1, keepdims=True)
    grid_grad = (out_grad_f + live * (inverse * upstream - grid_f * inverse**3 * centred)).astype(
        jnp.bfloat16
    )
    cells = groups * lax.axis_size("gy") * grid.shape[0] * grid.shape[1] * grid.shape[2]
    factor = 1.0 / math.sqrt(float(cells))
    return (block_out, grid_grad, first_total * factor, second_total * factor, gain_total * factor)


def solution(mesh):
    in_specs = (
        P("gx", "gy", "sa", None, None),
        P("gx", "gy", "sa", None),
        P("gx", "gy", "sa"),
        P(),
        P(),
        P(),
        P("gx", "gy", "sa", None),
    )
    out_specs = (P("gx", "gy", "sa", None), P("gx", "gy", "sa", None), P(), P(), P())
    return jax.shard_map(local, mesh=mesh, in_specs=in_specs, out_specs=out_specs, check_vma=False)
```

profile of v0, /device:TPU:1, one launch (start us, length us, event | category | flops | bytes accessed | tf_op | source)
XLA Modules:
  0.0 428.6 jit_solution(9511236412537976716)
XLA Ops:
  10.5 13.8 %all_to_all.18 = bf16[16,16,1]{1,2,0:T(2,128)(2,1)S(1)} all-to-all(bf16[16,16,1]{1,2,0:T(2,128)(2,1)S(1)} %convert_element_type.163), channel_id=1, replica_groups=mesh['gx'=8,'gy'=8,'sa'=2] {'gx','sa'}, dimensions={0} | all-to-all | bytes 1024 | tf_op jit(solution)/shard_map/all_to_all | solution.py:115
  24.9 1.2 fusion.57
  26.1 2.2 collective-permute-start.12
  28.3 1.3 collective-permute-start.13
  29.6 5.4 %convolution_convert_fusion = bf16[256,8192]{1,0:T(8,128)(2,1)} fusion(bf16[16,8,64,128]{3,2,1,0:T(8,128)(2,1)} %bitcast.1016, s32[128]{0:T(128)S(1)} %multiply_add_fusion), kind=kOutput, calls=%fused_computation | convolution fusion | flops 539000832 | bytes 6291968 | tf_op jit(solution)/shard_map/dot_general | solution.py:105
  35.0 5.6 %all-to-all-start.1 = ((bf16[16,16,8192]{2,1,0:T(8,128)(2,1)}), bf16[16,16,8192]{2,1,0:T(8,128)(2,1)}, u32[]{:S(2)}, u32[]{:S(2)}) async-start(bf16[16,16,8192]{2,1,0:T(8,128)(2,1)} %bitcast.1011), calls=%async_computation.1 | async-start | bytes 8388608 | tf_op jit(solution)/shard_map/all_to_all | solution.py:114
  41.0 6.4 %collective-permute-start.14 = (bf16[10,1,8,128]{3,1,2,0:T(2,128)(2,1)S(1)}, bf16[10,1,8,128]{3,1,2,0:T(2,128)(2,1)S(1)}, u32[]{:S(2)}, u32[]{:S(2)}) collective-permute-start(bf16[10,1,8,128]{3,1,2,0:T(2,128)(2,1)S(1)} %get-tuple-element.154), channel_id=1, source_target_pairs={{0,2},{2,4},{4,6},{6,8},{8,10},{10,12},{12,14},{1,3},{3,5},{5,7},{... | collective-permute-start | bytes 61448 | tf_op jit(solution)/shard_map/ppermute | solution.py:18
  47.4 1.9 collective-permute-start.15
  49.6 3.6 collective-permute-done.15
  53.2 1.3 collective-permute-start.16
  54.5 6.0 %collective-permute-start.17 = (bf16[10,18,1,128]{3,1,2,0:T(8,128)(2,1)S(1)}, bf16[10,18,1,128]{3,1,2,0:T(8,128)(2,1)S(1)}, u32[]{:S(2)}, u32[]{:S(2)}) collective-permute-start(bf16[10,18,1,128]{3,1,2,0:T(8,128)(2,1)S(1)} %get-tuple-element.138), channel_id=1, source_target_pairs={{0,1},{2,3},{4,5},{6,7},{8,9},{10,11},{12,13},{14,15},{16,17},{18,... | collective-permute-start | bytes 138248 | tf_op jit(solution)/shard_map/ppermute | solution.py:18
  61.7 32.9 %collective-permute-done.16 = bf16[10,18,1,128]{3,1,2,0:T(8,128)(2,1)S(1)} collective-permute-done((bf16[10,18,1,128]{3,1,2,0:T(8,128)(2,1)S(1)}, bf16[10,18,1,128]{3,1,2,0:T(8,128)(2,1)S(1)}, u32[]{:S(2)}, u32[]{:S(2)}) %collective-permute-start.16) | collective-permute-done | bytes 46112 | tf_op jit(solution)/shard_map/ppermute | solution.py:21
  105.7 2.8 fusion
  110.4 1.7 collective-permute-start
  112.1 1.3 collective-permute-start.1
  114.3 2.4 collective-permute-done.1
  116.8 8.0 %collective-permute-start.2 = (bf16[10,1,8,128]{3,1,2,0:T(2,128)(2,1)S(1)}, bf16[10,1,8,128]{3,1,2,0:T(2,128)(2,1)S(1)}, u32[]{:S(2)}, u32[]{:S(2)}) collective-permute-start(bf16[10,1,8,128]{3,1,2,0:T(2,128)(2,1)S(1)} %get-tuple-element.162), channel_id=1, source_target_pairs={{0,2},{2,4},{4,6},{6,8},{8,10},{10,12},{12,14},{1,3},{3,5},{5,7},{... | collective-permute-start | bytes 61448 | tf_op jit(solution)/shard_map/ppermute | solution.py:18
  124.8 1.9 collective-permute-start.3
  127.0 3.2 collective-permute-done.3
  130.2 1.3 collective-permute-start.4
  131.5 1.5 collective-permute-start.5
  134.1 3.9 collective-permute-done.5
  148.8 3.7 collective-permute-start.6
  152.5 1.5 collective-permute-start.7
  161.9 4.8 %collective-permute-start.18 = (bf16[1,16,8,128]{3,1,2,0:T(8,128)(2,1)S(1)}, bf16[1,16,8,128]{3,1,2,0:T(8,128)(2,1)S(1)}, u32[]{:S(2)}, u32[]{:S(2)}) collective-permute-start(bf16[1,16,8,128]{3,1,2,0:T(8,128)(2,1)S(1)} %get-tuple-element.166), channel_id=1, source_target_pairs={{0,16},{16,32},{32,48},{48,64},{64,80},{80,96},{96,112},{1,17},{17... | collective-permute-start | bytes 98312 | tf_op jit(solution)/shard_map/ppermute | solution.py:18
  166.7 1.3 collective-permute-start.19
  168.1 3.8 collective-permute-start.8
  171.9 1.9 collective-permute-start.9
  175.6 3.6 collective-permute-start.20
  179.3 1.9 collective-permute-start.21
  182.0 1.6 collective-permute-start.10
  183.7 1.3 collective-permute-start.11
  190.3 1.3 collective-permute-start.22
  191.6 7.0 %collective-permute-start.23 = (bf16[10,18,1,128]{3,1,2,0:T(8,128)(2,1)}, bf16[10,18,1,128]{3,1,2,0:T(8,128)(2,1)}, u32[]{:S(2)}, u32[]{:S(2)}) collective-permute-start(bf16[10,18,1,128]{3,1,2,0:T(8,128)(2,1)} %get-tuple-element.134), channel_id=1, source_target_pairs={{0,1},{2,3},{4,5},{6,7},{8,9},{10,11},{12,13},{14,15},{16,17},{18,... | collective-permute-start | bytes 138248 | tf_op jit(solution)/shard_map/ppermute | solution.py:18
  204.0 1.2 fusion.367
  206.1 1.3 fusion.366
  232.7 1.1 convolution_add_fusion.65
  234.7 1.7 copy.429
  236.5 1.8 copy.430
  238.3 1.7 copy.432
  240.0 1.7 copy.433
  241.7 1.7 copy.435
  244.2 1.7 copy.438
  246.9 1.3 maximum_maximum_fusion.3
  277.2 68.9 %psum.23 = f32[128]{0:T(128)S(1)} all-reduce(f32[128]{0:T(128)S(1)} %get-tuple-element.182), channel_id=1, replica_groups=mesh['gx'=8,'gy'=8,'sa'=2] {'gx','gy','sa'}, use_global_device_ids=true, to_apply=%region_9.10 | all-reduce | flops 128 | bytes 1024 | tf_op jit(solution)/shard_map/psum | solution.py:147
  346.6 70.2 %all-reduce.3.cloned.1.call-done = (f32[27,128,128]{2,1,0:T(8,128)}, f32[27,128,128]{2,1,0:T(8,128)}) async-done(((f32[27,128,128]{2,1,0:T(8,128)}, f32[27,128,128]{2,1,0:T(8,128)}), (f32[27,128,128]{2,1,0:T(8,128)}, f32[27,128,128]{2,1,0:T(8,128)})) %all-reduce.3.cloned.1.call-update) | async-done | bytes 3538960 | tf_op jit(solution)/shard_map/psum | solution.py:147
  416.8 3.1 broadcast_multiply_fusion
  419.8 1.4 broadcast_multiply_fusion.1
  (446 shorter events, 109.2 us)
Async XLA Ops:
  24.9 10.1 %copy-start.31 = (f32[8,16,8]{1,2,0:T(8,128)}, f32[8,16,8]{1,2,0:T(8,128)S(1)}, u32[]{:S(2)}) copy-start(f32[8,16,8]{1,2,0:T(8,128)S(1)} %copy.557) | copy-start | bytes 12292
  26.1 14.8 %collective-permute-start.12 = (bf16[1,16,8,128]{3,1,2,0:T(8,128)(2,1)S(1)}, bf16[1,16,8,128]{3,1,2,0:T(8,128)(2,1)S(1)}, u32[]{:S(2)}, u32[]{:S(2)}) collective-permute-start(bf16[1,16,8,128]{3,1,2,0:T(8,128)(2,1)S(1)} %get-tuple-element.170), channel_id=1, source_target_pairs={{0,16},{16,32},{32,48},{48,64},{64,80},{80,96},{96,112},{1,17},{17... | collective-permute-start | bytes 98312 | tf_op jit(solution)/shard_map/ppermute | solution.py:18
  28.3 12.7 %collective-permute-start.13 = (bf16[1,16,8,128]{3,1,2,0:T(8,128)(2,1)S(1)}, bf16[1,16,8,128]{3,1,2,0:T(8,128)(2,1)S(1)}, u32[]{:S(2)}, u32[]{:S(2)}) collective-permute-start(bf16[1,16,8,128]{3,1,2,0:T(8,128)(2,1)S(1)} %get-tuple-element.171), channel_id=1, source_target_pairs={{16,0},{32,16},{48,32},{64,48},{80,64},{96,80},{112,96},{17,1},{33... | collective-permute-start | bytes 98312 | tf_op jit(solution)/shard_map/ppermute | solution.py:21
  35.0 70.6 %all-to-all-start.1 = ((bf16[16,16,8192]{2,1,0:T(8,128)(2,1)}), bf16[16,16,8192]{2,1,0:T(8,128)(2,1)}, u32[]{:S(2)}, u32[]{:S(2)}) async-start(bf16[16,16,8192]{2,1,0:T(8,128)(2,1)} %bitcast.1011), calls=%async_computation.1 | async-start | bytes 8388608 | tf_op jit(solution)/shard_map/all_to_all | solution.py:114
  40.6 376.1 %all-reduce.3.cloned.1.call-start = ((), (), s32[]{:S(2)}) async-start(), calls=%async_computation.2 | async-start | bytes 7077888 | tf_op jit(solution)/shard_map/psum | solution.py:147
  41.0 8.5 %collective-permute-start.14 = (bf16[10,1,8,128]{3,1,2,0:T(2,128)(2,1)S(1)}, bf16[10,1,8,128]{3,1,2,0:T(2,128)(2,1)S(1)}, u32[]{:S(2)}, u32[]{:S(2)}) collective-permute-start(bf16[10,1,8,128]{3,1,2,0:T(2,128)(2,1)S(1)} %get-tuple-element.154), channel_id=1, source_target_pairs={{0,2},{2,4},{4,6},{6,8},{8,10},{10,12},{12,14},{1,3},{3,5},{5,7},{... | collective-permute-start | bytes 61448 | tf_op jit(solution)/shard_map/ppermute | solution.py:18
  47.4 5.7 %collective-permute-start.15 = (bf16[10,1,8,128]{3,1,2,0:T(2,128)(2,1)S(1)}, bf16[10,1,8,128]{3,1,2,0:T(2,128)(2,1)S(1)}, u32[]{:S(2)}, u32[]{:S(2)}) collective-permute-start(bf16[10,1,8,128]{3,1,2,0:T(2,128)(2,1)S(1)} %get-tuple-element.155), channel_id=1, source_target_pairs={{2,0},{4,2},{6,4},{8,6},{10,8},{12,10},{14,12},{3,1},{5,3},{7,5},{... | collective-permute-start | bytes 61448 | tf_op jit(solution)/shard_map/ppermute | solution.py:21
  53.2 41.4 %collective-permute-start.16 = (bf16[10,18,1,128]{3,1,2,0:T(8,128)(2,1)S(1)}, bf16[10,18,1,128]{3,1,2,0:T(8,128)(2,1)S(1)}, u32[]{:S(2)}, u32[]{:S(2)}) collective-permute-start(bf16[10,18,1,128]{3,1,2,0:T(8,128)(2,1)S(1)} %get-tuple-element.139), channel_id=1, source_target_pairs={{1,0},{3,2},{5,4},{7,6},{9,8},{11,10},{13,12},{15,14},{17,16},{19,... | collective-permute-start | bytes 138248 | tf_op jit(solution)/shard_map/ppermute | solution.py:21
  54.5 40.1 %collective-permute-start.17 = (bf16[10,18,1,128]{3,1,2,0:T(8,128)(2,1)S(1)}, bf16[10,18,1,128]{3,1,2,0:T(8,128)(2,1)S(1)}, u32[]{:S(2)}, u32[]{:S(2)}) collective-permute-start(bf16[10,18,1,128]{3,1,2,0:T(8,128)(2,1)S(1)} %get-tuple-element.138), channel_id=1, source_target_pairs={{0,1},{2,3},{4,5},{6,7},{8,9},{10,11},{12,13},{14,15},{16,17},{18,... | collective-permute-start | bytes 138248 | tf_op jit(solution)/shard_map/ppermute | solution.py:18
  109.6 4.7 %copy-start.34 = (f32[8,16,8]{1,2,0:T(8,128)}, f32[8,16,8]{1,2,0:T(8,128)S(1)}, u32[]{:S(2)}) copy-start(f32[8,16,8]{1,2,0:T(8,128)S(1)} %copy.558) | copy-start | bytes 12292
  110.4 4.0 collective-permute-start
  112.1 4.7 %collective-permute-start.1 = (bf16[1,16,8,128]{3,1,2,0:T(8,128)(2,1)S(1)}, bf16[1,16,8,128]{3,1,2,0:T(8,128)(2,1)S(1)}, u32[]{:S(2)}, u32[]{:S(2)}) collective-permute-start(bf16[1,16,8,128]{3,1,2,0:T(8,128)(2,1)S(1)} %get-tuple-element.179), channel_id=1, source_target_pairs={{16,0},{32,16},{48,32},{64,48},{80,64},{96,80},{112,96},{17,1},{33... | collective-permute-start | bytes 98312 | tf_op jit(solution)/shard_map/ppermute | solution.py:21
  114.3 23.7 %copy-start.29 = (bf16[1,16,8,128]{3,1,2,0:T(8,128)(2,1)}, bf16[1,16,8,128]{3,1,2,0:T(8,128)(2,1)S(1)}, u32[]{:S(2)}) copy-start(bf16[1,16,8,128]{3,1,2,0:T(8,128)(2,1)S(1)} %collective-permute-done) | copy-start | bytes 98308
  116.8 10.2 %collective-permute-start.2 = (bf16[10,1,8,128]{3,1,2,0:T(2,128)(2,1)S(1)}, bf16[10,1,8,128]{3,1,2,0:T(2,128)(2,1)S(1)}, u32[]{:S(2)}, u32[]{:S(2)}) collective-permute-start(bf16[10,1,8,128]{3,1,2,0:T(2,128)(2,1)S(1)} %get-tuple-element.162), channel_id=1, source_target_pairs={{0,2},{2,4},{4,6},{6,8},{8,10},{10,12},{12,14},{1,3},{3,5},{5,7},{... | collective-permute-start | bytes 61448 | tf_op jit(solution)/shard_map/ppermute | solution.py:18
  124.8 5.3 %collective-permute-start.3 = (bf16[10,1,8,128]{3,1,2,0:T(2,128)(2,1)S(1)}, bf16[10,1,8,128]{3,1,2,0:T(2,128)(2,1)S(1)}, u32[]{:S(2)}, u32[]{:S(2)}) collective-permute-start(bf16[10,1,8,128]{3,1,2,0:T(2,128)(2,1)S(1)} %get-tuple-element.163), channel_id=1, source_target_pairs={{2,0},{4,2},{6,4},{8,6},{10,8},{12,10},{14,12},{3,1},{5,3},{7,5},{... | collective-permute-start | bytes 61448 | tf_op jit(solution)/shard_map/ppermute | solution.py:21
  130.2 3.9 collective-permute-start.4
  131.5 6.5 %collective-permute-start.5 = (bf16[10,18,1,128]{3,1,2,0:T(8,128)(2,1)S(1)}, bf16[10,18,1,128]{3,1,2,0:T(8,128)(2,1)S(1)}, u32[]{:S(2)}, u32[]{:S(2)}) collective-permute-start(bf16[10,18,1,128]{3,1,2,0:T(8,128)(2,1)S(1)} %get-tuple-element.146), channel_id=1, source_target_pairs={{1,0},{3,2},{5,4},{7,6},{9,8},{11,10},{13,12},{15,14},{17,16},{19,... | collective-permute-start | bytes 138248 | tf_op jit(solution)/shard_map/ppermute | solution.py:21
  148.4 9.5 %copy-start.43 = (bf16[1024,128]{1,0:T(8,128)(2,1)}, bf16[1024,128]{1,0:T(8,128)(2,1)S(1)}, u32[]{:S(2)}) copy-start(bf16[1024,128]{1,0:T(8,128)(2,1)S(1)} %get-tuple-element.180) | copy-start | bytes 786436
  148.8 19.1 %collective-permute-start.6 = (bf16[1,16,8,128]{3,1,2,0:T(8,128)(2,1)S(1)}, bf16[1,16,8,128]{3,1,2,0:T(8,128)(2,1)S(1)}, u32[]{:S(2)}, u32[]{:S(2)}) collective-permute-start(bf16[1,16,8,128]{3,1,2,0:T(8,128)(2,1)S(1)} %get-tuple-element.174), channel_id=1, source_target_pairs={{0,16},{16,32},{32,48},{48,64},{64,80},{80,96},{96,112},{1,17},{17... | collective-permute-start | bytes 98312 | tf_op jit(solution)/shard_map/ppermute | solution.py:18
  152.5 15.4 %collective-permute-start.7 = (bf16[1,16,8,128]{3,1,2,0:T(8,128)(2,1)S(1)}, bf16[1,16,8,128]{3,1,2,0:T(8,128)(2,1)S(1)}, u32[]{:S(2)}, u32[]{:S(2)}) collective-permute-start(bf16[1,16,8,128]{3,1,2,0:T(8,128)(2,1)S(1)} %get-tuple-element.175), channel_id=1, source_target_pairs={{16,0},{32,16},{48,32},{64,48},{80,64},{96,80},{112,96},{17,1},{33... | collective-permute-start | bytes 98312 | tf_op jit(solution)/shard_map/ppermute | solution.py:21
  161.8 13.0 %copy-start.4 = (f32[27,128,128]{2,1,0:T(8,128)}, f32[27,128,128]{2,1,0:T(8,128)S(1)}, u32[]{:S(2)}) copy-start(f32[27,128,128]{2,1,0:T(8,128)S(1)} %fusion.32) | copy-start | bytes 5308420
  161.9 12.0 %collective-permute-start.18 = (bf16[1,16,8,128]{3,1,2,0:T(8,128)(2,1)S(1)}, bf16[1,16,8,128]{3,1,2,0:T(8,128)(2,1)S(1)}, u32[]{:S(2)}, u32[]{:S(2)}) collective-permute-start(bf16[1,16,8,128]{3,1,2,0:T(8,128)(2,1)S(1)} %get-tuple-element.166), channel_id=1, source_target_pairs={{0,16},{16,32},{32,48},{48,64},{64,80},{80,96},{96,112},{1,17},{17... | collective-permute-start | bytes 98312 | tf_op jit(solution)/shard_map/ppermute | solution.py:18
  166.7 7.2 %collective-permute-start.19 = (bf16[1,16,8,128]{3,1,2,0:T(8,128)(2,1)S(1)}, bf16[1,16,8,128]{3,1,2,0:T(8,128)(2,1)S(1)}, u32[]{:S(2)}, u32[]{:S(2)}) collective-permute-start(bf16[1,16,8,128]{3,1,2,0:T(8,128)(2,1)S(1)} %get-tuple-element.167), channel_id=1, source_target_pairs={{16,0},{32,16},{48,32},{64,48},{80,64},{96,80},{112,96},{17,1},{33... | collective-permute-start | bytes 98312 | tf_op jit(solution)/shard_map/ppermute | solution.py:21
  168.1 13.9 %collective-permute-start.8 = (bf16[10,1,8,128]{3,1,2,0:T(2,128)(2,1)S(1)}, bf16[10,1,8,128]{3,1,2,0:T(2,128)(2,1)S(1)}, u32[]{:S(2)}, u32[]{:S(2)}) collective-permute-start(bf16[10,1,8,128]{3,1,2,0:T(2,128)(2,1)S(1)} %get-tuple-element.158), channel_id=1, source_target_pairs={{0,2},{2,4},{4,6},{6,8},{8,10},{10,12},{12,14},{1,3},{3,5},{5,7},{... | collective-permute-start | bytes 61448 | tf_op jit(solution)/shard_map/ppermute | solution.py:18
  171.9 10.1 %collective-permute-start.9 = (bf16[10,1,8,128]{3,1,2,0:T(2,128)(2,1)S(1)}, bf16[10,1,8,128]{3,1,2,0:T(2,128)(2,1)S(1)}, u32[]{:S(2)}, u32[]{:S(2)}) collective-permute-start(bf16[10,1,8,128]{3,1,2,0:T(2,128)(2,1)S(1)} %get-tuple-element.159), channel_id=1, source_target_pairs={{2,0},{4,2},{6,4},{8,6},{10,8},{12,10},{14,12},{3,1},{5,3},{7,5},{... | collective-permute-start | bytes 61448 | tf_op jit(solution)/shard_map/ppermute | solution.py:21
  173.9 15.7 %copy-start.27 = (bf16[1,16,8,128]{3,1,2,0:T(8,128)(2,1)}, bf16[1,16,8,128]{3,1,2,0:T(8,128)(2,1)S(1)}, u32[]{:S(2)}) copy-start(bf16[1,16,8,128]{3,1,2,0:T(8,128)(2,1)S(1)} %collective-permute-done.19) | copy-start | bytes 98308
  175.6 12.6 %collective-permute-start.20 = (bf16[10,1,8,128]{3,1,2,0:T(2,128)(2,1)S(1)}, bf16[10,1,8,128]{3,1,2,0:T(2,128)(2,1)S(1)}, u32[]{:S(2)}, u32[]{:S(2)}) collective-permute-start(bf16[10,1,8,128]{3,1,2,0:T(2,128)(2,1)S(1)} %get-tuple-element.150), channel_id=1, source_target_pairs={{0,2},{2,4},{4,6},{6,8},{8,10},{10,12},{12,14},{1,3},{3,5},{5,7},{... | collective-permute-start | bytes 61448 | tf_op jit(solution)/shard_map/ppermute | solution.py:18
  179.3 8.9 %collective-permute-start.21 = (bf16[10,1,8,128]{3,1,2,0:T(2,128)(2,1)S(1)}, bf16[10,1,8,128]{3,1,2,0:T(2,128)(2,1)S(1)}, u32[]{:S(2)}, u32[]{:S(2)}) collective-permute-start(bf16[10,1,8,128]{3,1,2,0:T(2,128)(2,1)S(1)} %get-tuple-element.151), channel_id=1, source_target_pairs={{2,0},{4,2},{6,4},{8,6},{10,8},{12,10},{14,12},{3,1},{5,3},{7,5},{... | collective-permute-start | bytes 61448 | tf_op jit(solution)/shard_map/ppermute | solution.py:21
  182.0 20.6 %collective-permute-start.10 = (bf16[10,18,1,128]{3,1,2,0:T(8,128)(2,1)S(1)}, bf16[10,18,1,128]{3,1,2,0:T(8,128)(2,1)S(1)}, u32[]{:S(2)}, u32[]{:S(2)}) collective-permute-start(bf16[10,18,1,128]{3,1,2,0:T(8,128)(2,1)S(1)} %get-tuple-element.143), channel_id=1, source_target_pairs={{0,1},{2,3},{4,5},{6,7},{8,9},{10,11},{12,13},{14,15},{16,17},{18,... | collective-permute-start | bytes 138248 | tf_op jit(solution)/shard_map/ppermute | solution.py:18
  183.7 18.9 %collective-permute-start.11 = (bf16[10,18,1,128]{3,1,2,0:T(8,128)(2,1)S(1)}, bf16[10,18,1,128]{3,1,2,0:T(8,128)(2,1)S(1)}, u32[]{:S(2)}, u32[]{:S(2)}) collective-permute-start(bf16[10,18,1,128]{3,1,2,0:T(8,128)(2,1)S(1)} %get-tuple-element.142), channel_id=1, source_target_pairs={{1,0},{3,2},{5,4},{7,6},{9,8},{11,10},{13,12},{15,14},{17,16},{19,... | collective-permute-start | bytes 138248 | tf_op jit(solution)/shard_map/ppermute | solution.py:21
  190.3 56.5 %collective-permute-start.22 = (bf16[10,18,1,128]{3,1,2,0:T(8,128)(2,1)}, bf16[10,18,1,128]{3,1,2,0:T(8,128)(2,1)}, u32[]{:S(2)}, u32[]{:S(2)}) collective-permute-start(bf16[10,18,1,128]{3,1,2,0:T(8,128)(2,1)} %get-tuple-element.135), channel_id=1, source_target_pairs={{1,0},{3,2},{5,4},{7,6},{9,8},{11,10},{13,12},{15,14},{17,16},{19,... | collective-permute-start | bytes 138248 | tf_op jit(solution)/shard_map/ppermute | solution.py:21
  191.6 55.3 %collective-permute-start.23 = (bf16[10,18,1,128]{3,1,2,0:T(8,128)(2,1)}, bf16[10,18,1,128]{3,1,2,0:T(8,128)(2,1)}, u32[]{:S(2)}, u32[]{:S(2)}) collective-permute-start(bf16[10,18,1,128]{3,1,2,0:T(8,128)(2,1)} %get-tuple-element.134), channel_id=1, source_target_pairs={{0,1},{2,3},{4,5},{6,7},{8,9},{10,11},{12,13},{14,15},{16,17},{18,... | collective-permute-start | bytes 138248 | tf_op jit(solution)/shard_map/ppermute | solution.py:18
  236.5 10.3 %copy-start.5 = (bf16[8,16,8,128]{3,1,2,0:T(8,128)(2,1)S(1)}, bf16[8,16,8,128]{3,1,2,0:T(8,128)(2,1)}, u32[]{:S(2)}) copy-start(bf16[8,16,8,128]{3,1,2,0:T(8,128)(2,1)} %get-tuple-element.72) | copy-start | bytes 786436
  238.3 8.6 %copy-start.28 = (bf16[1,16,8,128]{3,1,2,0:T(8,128)(2,1)S(1)}, bf16[1,16,8,128]{3,1,2,0:T(8,128)(2,1)}, u32[]{:S(2)}) copy-start(bf16[1,16,8,128]{3,1,2,0:T(8,128)(2,1)} %copy-done.27) | copy-start | bytes 98308
  238.3 8.6 %copy-start.39 = (bf16[10,1,8,128]{3,1,2,0:T(2,128)(2,1)S(1)}, bf16[10,1,8,128]{3,1,2,0:T(2,128)(2,1)}, u32[]{:S(2)}) copy-start(bf16[10,1,8,128]{3,1,2,0:T(2,128)(2,1)} %copy-done.38) | copy-start | bytes 61444
  238.3 8.6 %copy-start.41 = (bf16[10,1,8,128]{3,1,2,0:T(2,128)(2,1)S(1)}, bf16[10,1,8,128]{3,1,2,0:T(2,128)(2,1)}, u32[]{:S(2)}) copy-start(bf16[10,1,8,128]{3,1,2,0:T(2,128)(2,1)} %copy-done.40) | copy-start | bytes 61444
  260.4 3.1 copy-start.9
  261.5 3.1 copy-start.23
  262.5 3.1 copy-start.22
  263.6 3.1 copy-start.8
  264.6 3.1 copy-start.21
  265.6 3.1 copy-start.20
  266.7 3.1 copy-start.6
  267.7 3.1 copy-start.18
  268.7 3.1 copy-start.19
  269.8 3.1 copy-start.7
  271.8 3.0 copy-start.26
  416.8 3.1 copy-start.3
  (25 other events, 35.3 us)
Sparse Core Ops, SparseCore 0:
  260.5 156.2 all-reduce.2
where the time goes:
time: 434 us; the launch traced here: 429 us
  waiting for transfers between devices  116 us (27%)
  blocking collectives  82.7 us (19%)
  matrix products  76.1 us (18%)
  starting transfers between devices  74.1 us (17%)
  local copies, waits for them, and re-layouts  43.7 us (10%)
  other arithmetic  18.5 us (4%)
  between operations  17.2 us (4%)
    psum x1, waiting for transfers between devices, local(): lax.psum((first_grad, second_grad, gain_grad), ('gx', 'gy', 'sa'))  70.2 us
    psum x1, blocking collectives, local(): lax.psum((first_grad, second_grad, gain_grad), ('gx', 'gy', 'sa'))  68.9 us
    ppermute x12, starting transfers between devices, extended(): lax.ppermute(lax.slice_in_dim(block, block.shape[dim] - width, None, axis...  50.1 us
    ppermute x12, waiting for transfers between devices, extended(): lax.ppermute(lax.slice_in_dim(block, 0, width, axis=dim), axis, backward)  46 us
    dot_general x54, matrix products, weight_grads(): lax.dot_general(window.reshape(-1, padded.shape[3]), grad_rows, (((0,), (...  31.9 us
    dot_general x54, matrix products, apply_conv(): jnp.dot(window.reshape(-1, channels), weights[offset], preferred_element_...  22.5 us
    slice x58, local copies, waits for them, and re-layouts, apply_conv(): padded[along_x:along_x + extent_x, along_y:along_y + extent_y, along_z:al...  22 us
    ppermute x12, starting transfers between devices, extended(): lax.ppermute(lax.slice_in_dim(block, 0, width, axis=dim), axis, backward)  18.4 us
  transfers between devices with their start and end apart: 26, of which 6 were waited for; matrix products, arithmetic and copies ran while one was open for 23% of the time, Pallas kernels for 0%

commit v1 on v0

--- a/solution.py
+++ b/solution.py
@@ -145,7 +145,7 @@
     normed_grad = live * transposed_conv(pre_pad, conv_first)
     gain_grad = jnp.sum((normed_grad * grid_f * inverse).reshape(-1, channels), axis=0)
     first_total, second_total, gain_total = lax.psum(
-        (first_grad, second_grad, gain_grad), ("gx", "gy", "sa")
+        lax.psum((first_grad, second_grad, gain_grad), "gx"), ("gy", "sa")
     )
     upstream = normed_grad * norm_gain
     centred = jnp.mean(grid_f * upstream, axis=-1, keepdims=True)

time: 434 us -> 624 us (1.44)
  waiting for transfers between devices: 116 us -> 315 us
  blocking collectives: 82.7 us -> 68.2 us
  local copies, waits for them, and re-layouts: 43.7 us -> 56.6 us
  matrix products: 76.1 us -> 68.6 us
    psum x1 -> x2, waiting for transfers between devices: 70.2 us -> 270 us  [the longest x1 156 us: local(): lax.psum((first_grad, second_grad, gain_grad), 'gx')]
    psum x1 -> x2, blocking collectives: 68.9 us -> 54.4 us  [the longest x1 39.9 us: local(): lax.psum(lax.psum((first_grad, second_grad, gain_grad), 'gx'), ('gy', 'sa'))]
    dot_general x54, matrix products: 22.5 us -> 14.1 us  [apply_conv(): jnp.dot(window.reshape(-1, channels), weights[offset], preferred_element_...]
    slice x58, local copies, waits for them, and re-layouts: 22 us -> 29.8 us  [apply_conv(): padded[along_x:along_x + extent_x, along_y:along_y + extent_y, along_z:al...]
  transfers between devices with their start and end apart: 26 -> 27, of which waited for: 6 -> 7; matrix products, arithmetic and copies ran while one was open for 23% -> 16% of each run, Pallas kernels for 0% -> 0%
where the time goes in v1:
time: 624 us; the launch traced here: 618 us
  waiting for transfers between devices  315 us (50%)
  starting transfers between devices  74.2 us (12%)
  matrix products  68.6 us (11%)
  blocking collectives  68.2 us (11%)
  local copies, waits for them, and re-layouts  56.6 us (9%)
  other arithmetic  18.5 us (3%)
  between operations  16.9 us (3%)
    psum x1, waiting for transfers between devices, local(): lax.psum((first_grad, second_grad, gain_grad), 'gx')  156 us
    psum x1, waiting for transfers between devices, local(): lax.psum(lax.psum((first_grad, second_grad, gain_grad), 'gx'), ('gy', 'sa'))  114 us
    ppermute x12, starting transfers between devices, extended(): lax.ppermute(lax.slice_in_dim(block, block.shape[dim] - width, None, axis...  50.1 us
    ppermute x12, waiting for transfers between devices, extended(): lax.ppermute(lax.slice_in_dim(block, 0, width, axis=dim), axis, backward)  45.2 us
    psum x1, blocking collectives, local(): lax.psum(lax.psum((first_grad, second_grad, gain_grad), 'gx'), ('gy', 'sa'))  39.9 us
    dot_general x54, matrix products, weight_grads(): lax.dot_general(window.reshape(-1, padded.shape[3]), grad_rows, (((0,), (...  31.8 us
    slice x58, local copies, waits for them, and re-layouts, apply_conv(): padded[along_x:along_x + extent_x, along_y:along_y + extent_y, along_z:al...  29.8 us
    ppermute x12, starting transfers between devices, extended(): lax.ppermute(lax.slice_in_dim(block, 0, width, axis=dim), axis, backward)  18.4 us
  transfers between devices with their start and end apart: 27, of which 7 were waited for; matrix products, arithmetic and copies ran while one was open for 16% of the time, Pallas kernels for 0%

profile of v1, /device:TPU:1, one launch (start us, length us, event | category | flops | bytes accessed | tf_op | source)
XLA Modules:
  0.0 618.0 jit_solution(11325675790951486368)
XLA Ops:
  10.5 13.8 %all_to_all.18 = bf16[16,16,1]{1,2,0:T(2,128)(2,1)S(1)} all-to-all(bf16[16,16,1]{1,2,0:T(2,128)(2,1)S(1)} %convert_element_type.163), channel_id=1, replica_groups=mesh['gx'=8,'gy'=8,'sa'=2] {'gx','sa'}, dimensions={0} | all-to-all | bytes 1024 | tf_op jit(solution)/shard_map/all_to_all | solution.py:115
  26.1 2.2 collective-permute-start.12
  28.3 1.3 collective-permute-start.13
  29.6 5.4 convolution_convert_fusion
  35.0 5.6 all-to-all-start.1
  41.0 6.4 %collective-permute-start.14 = (bf16[10,1,8,128]{3,1,2,0:T(2,128)(2,1)S(1)}, bf16[10,1,8,128]{3,1,2,0:T(2,128)(2,1)S(1)}, u32[]{:S(2)}, u32[]{:S(2)}) collective-permute-start(bf16[10,1,8,128]{3,1,2,0:T(2,128)(2,1)S(1)} %get-tuple-element.156), channel_id=1, source_target_pairs={{0,2},{2,4},{4,6},{6,8},{8,10},{10,12},{12,14},{1,3},{3,5},{5,7},{... | collective-permute-start | bytes 61448 | tf_op jit(solution)/shard_map/ppermute | solution.py:18
  47.4 1.9 collective-permute-start.15
  49.6 3.6 collective-permute-done.15
  53.2 1.3 collective-permute-start.16
  54.5 6.0 collective-permute-start.17
  61.7 33.0 %collective-permute-done.16 = bf16[10,18,1,128]{3,1,2,0:T(8,128)(2,1)S(1)} collective-permute-done((bf16[10,18,1,128]{3,1,2,0:T(8,128)(2,1)S(1)}, bf16[10,18,1,128]{3,1,2,0:T(8,128)(2,1)S(1)}, u32[]{:S(2)}, u32[]{:S(2)}) %collective-permute-start.16) | collective-permute-done | bytes 46112 | tf_op jit(solution)/shard_map/ppermute | solution.py:21
  105.7 2.8 fusion
  110.4 1.6 collective-permute-start
  112.0 1.3 collective-permute-start.1
  115.1 1.6 collective-permute-done.1
  116.8 8.1 %collective-permute-start.2 = (bf16[10,1,8,128]{3,1,2,0:T(2,128)(2,1)S(1)}, bf16[10,1,8,128]{3,1,2,0:T(2,128)(2,1)S(1)}, u32[]{:S(2)}, u32[]{:S(2)}) collective-permute-start(bf16[10,1,8,128]{3,1,2,0:T(2,128)(2,1)S(1)} %get-tuple-element.164), channel_id=1, source_target_pairs={{0,2},{2,4},{4,6},{6,8},{8,10},{10,12},{12,14},{1,3},{3,5},{5,7},{... | collective-permute-start | bytes 61448 | tf_op jit(solution)/shard_map/ppermute | solution.py:18
  124.9 1.9 collective-permute-start.3
  127.0 3.2 collective-permute-done.3
  130.3 1.3 collective-permute-start.4
  131.6 1.5 collective-permute-start.5
  134.2 3.9 collective-permute-done.5
  149.4 3.7 collective-permute-start.6
  153.1 1.5 collective-permute-start.7
  162.4 4.7 collective-permute-start.18
  167.1 1.3 collective-permute-start.19
  168.5 3.8 collective-permute-start.8
  172.3 1.9 collective-permute-start.9
  176.8 3.6 collective-permute-start.20
  180.4 1.9 collective-permute-start.21
  183.2 1.7 collective-permute-start.10
  184.9 1.3 collective-permute-start.11
  193.7 1.3 collective-permute-start.22
  194.9 6.9 %collective-permute-start.23 = (bf16[10,18,1,128]{3,1,2,0:T(8,128)(2,1)}, bf16[10,18,1,128]{3,1,2,0:T(8,128)(2,1)}, u32[]{:S(2)}, u32[]{:S(2)}) collective-permute-start(bf16[10,18,1,128]{3,1,2,0:T(8,128)(2,1)} %get-tuple-element.136), channel_id=1, source_target_pairs={{0,1},{2,3},{4,5},{6,7},{8,9},{10,11},{12,13},{14,15},{16,17},{18,... | collective-permute-start | bytes 138248 | tf_op jit(solution)/shard_map/ppermute | solution.py:18
  207.4 1.4 fusion.367
  209.7 1.5 fusion.366
  233.0 1.8 fusion.141
  235.7 1.8 copy.418
  237.5 1.8 copy.419
  239.3 1.8 copy.421
  241.1 1.8 copy.422
  253.0 1.3 maximum_maximum_fusion.3
  269.0 1.2 convolution_add_fusion.76
  274.3 155.7 %all-reduce.7.cloned.1.call-done = (f32[27,128,128]{2,1,0:T(8,128)}, f32[27,128,128]{2,1,0:T(8,128)}) async-done(((f32[27,128,128]{2,1,0:T(8,128)}, f32[27,128,128]{2,1,0:T(8,128)}), (f32[27,128,128]{2,1,0:T(8,128)}, f32[27,128,128]{2,1,0:T(8,128)})) %all-reduce.7.cloned.1.call-update) | async-done | bytes 3538960 | tf_op jit(solution)/shard_map/psum | solution.py:148
  437.3 14.5 %psum.46 = f32[128]{0:T(128)S(1)} all-reduce(f32[128]{0:T(128)S(1)} %copy-done.70), channel_id=1, replica_groups=mesh['gx'=8,'gy'=8,'sa'=2] {'gx'}, use_global_device_ids=true, to_apply=%region_11.12 | all-reduce | flops 128 | bytes 1024 | tf_op jit(solution)/shard_map/psum | solution.py:148
  451.8 39.9 %psum.47 = f32[128]{0:T(128)S(1)} all-reduce(f32[128]{0:T(128)S(1)} %psum.46), channel_id=1, replica_groups=mesh['gx'=8,'gy'=8,'sa'=2] {'gy','sa'}, use_global_device_ids=true, to_apply=%region_12.13 | all-reduce | flops 128 | bytes 1024 | tf_op jit(solution)/shard_map/psum | solution.py:147
  492.2 114.0 %all-reduce.5.cloned.1.call-done = (f32[27,128,128]{2,1,0:T(8,128)}, f32[27,128,128]{2,1,0:T(8,128)}) async-done(((f32[27,128,128]{2,1,0:T(8,128)}, f32[27,128,128]{2,1,0:T(8,128)}), (f32[27,128,128]{2,1,0:T(8,128)}, f32[27,128,128]{2,1,0:T(8,128)})) %all-reduce.5.cloned.1.call-update) | async-done | bytes 3538960 | tf_op jit(solution)/shard_map/psum | solution.py:147
  606.2 3.1 broadcast_multiply_fusion
  609.3 1.4 broadcast_multiply_fusion.1
  (498 shorter events, 116.7 us)
Async XLA Ops:
  24.9 10.1 %copy-start.55 = (f32[8,16,8]{1,2,0:T(8,128)}, f32[8,16,8]{1,2,0:T(8,128)S(1)}, u32[]{:S(2)}) copy-start(f32[8,16,8]{1,2,0:T(8,128)S(1)} %copy.557) | copy-start | bytes 12292
  26.1 14.8 %collective-permute-start.12 = (bf16[1,16,8,128]{3,1,2,0:T(8,128)(2,1)S(1)}, bf16[1,16,8,128]{3,1,2,0:T(8,128)(2,1)S(1)}, u32[]{:S(2)}, u32[]{:S(2)}) collective-permute-start(bf16[1,16,8,128]{3,1,2,0:T(8,128)(2,1)S(1)} %get-tuple-element.172), channel_id=1, source_target_pairs={{0,16},{16,32},{32,48},{48,64},{64,80},{80,96},{96,112},{1,17},{17... | collective-permute-start | bytes 98312 | tf_op jit(solution)/shard_map/ppermute | solution.py:18
  28.3 12.6 %collective-permute-start.13 = (bf16[1,16,8,128]{3,1,2,0:T(8,128)(2,1)S(1)}, bf16[1,16,8,128]{3,1,2,0:T(8,128)(2,1)S(1)}, u32[]{:S(2)}, u32[]{:S(2)}) collective-permute-start(bf16[1,16,8,128]{3,1,2,0:T(8,128)(2,1)S(1)} %get-tuple-element.173), channel_id=1, source_target_pairs={{16,0},{32,16},{48,32},{64,48},{80,64},{96,80},{112,96},{17,1},{33... | collective-permute-start | bytes 98312 | tf_op jit(solution)/shard_map/ppermute | solution.py:21
  35.0 70.7 %all-to-all-start.1 = ((bf16[16,16,8192]{2,1,0:T(8,128)(2,1)}), bf16[16,16,8192]{2,1,0:T(8,128)(2,1)}, u32[]{:S(2)}, u32[]{:S(2)}) async-start(bf16[16,16,8192]{2,1,0:T(8,128)(2,1)} %bitcast.1011), calls=%async_computation.1 | async-start | bytes 8388608 | tf_op jit(solution)/shard_map/all_to_all | solution.py:114
  40.6 389.4 %all-reduce.7.cloned.1.call-start = ((), (), s32[]{:S(2)}) async-start(), calls=%async_computation.3 | async-start | bytes 7077888 | tf_op jit(solution)/shard_map/psum | solution.py:148
  41.0 8.5 %collective-permute-start.14 = (bf16[10,1,8,128]{3,1,2,0:T(2,128)(2,1)S(1)}, bf16[10,1,8,128]{3,1,2,0:T(2,128)(2,1)S(1)}, u32[]{:S(2)}, u32[]{:S(2)}) collective-permute-start(bf16[10,1,8,128]{3,1,2,0:T(2,128)(2,1)S(1)} %get-tuple-element.156), channel_id=1, source_target_pairs={{0,2},{2,4},{4,6},{6,8},{8,10},{10,12},{12,14},{1,3},{3,5},{5,7},{... | collective-permute-start | bytes 61448 | tf_op jit(solution)/shard_map/ppermute | solution.py:18
  47.4 5.7 collective-permute-start.15
  53.2 41.4 %collective-permute-start.16 = (bf16[10,18,1,128]{3,1,2,0:T(8,128)(2,1)S(1)}, bf16[10,18,1,128]{3,1,2,0:T(8,128)(2,1)S(1)}, u32[]{:S(2)}, u32[]{:S(2)}) collective-permute-start(bf16[10,18,1,128]{3,1,2,0:T(8,128)(2,1)S(1)} %get-tuple-element.141), channel_id=1, source_target_pairs={{1,0},{3,2},{5,4},{7,6},{9,8},{11,10},{13,12},{15,14},{17,16},{19,... | collective-permute-start | bytes 138248 | tf_op jit(solution)/shard_map/ppermute | solution.py:21
  54.5 40.1 %collective-permute-start.17 = (bf16[10,18,1,128]{3,1,2,0:T(8,128)(2,1)S(1)}, bf16[10,18,1,128]{3,1,2,0:T(8,128)(2,1)S(1)}, u32[]{:S(2)}, u32[]{:S(2)}) collective-permute-start(bf16[10,18,1,128]{3,1,2,0:T(8,128)(2,1)S(1)} %get-tuple-element.140), channel_id=1, source_target_pairs={{0,1},{2,3},{4,5},{6,7},{8,9},{10,11},{12,13},{14,15},{16,17},{18,... | collective-permute-start | bytes 138248 | tf_op jit(solution)/shard_map/ppermute | solution.py:18
  109.7 5.4 copy-start.58
  110.4 4.7 collective-permute-start
  112.0 4.7 collective-permute-start.1
  115.1 22.9 %copy-start.53 = (bf16[1,16,8,128]{3,1,2,0:T(8,128)(2,1)}, bf16[1,16,8,128]{3,1,2,0:T(8,128)(2,1)S(1)}, u32[]{:S(2)}) copy-start(bf16[1,16,8,128]{3,1,2,0:T(8,128)(2,1)S(1)} %collective-permute-done) | copy-start | bytes 98308
  116.8 10.2 %collective-permute-start.2 = (bf16[10,1,8,128]{3,1,2,0:T(2,128)(2,1)S(1)}, bf16[10,1,8,128]{3,1,2,0:T(2,128)(2,1)S(1)}, u32[]{:S(2)}, u32[]{:S(2)}) collective-permute-start(bf16[10,1,8,128]{3,1,2,0:T(2,128)(2,1)S(1)} %get-tuple-element.164), channel_id=1, source_target_pairs={{0,2},{2,4},{4,6},{6,8},{8,10},{10,12},{12,14},{1,3},{3,5},{5,7},{... | collective-permute-start | bytes 61448 | tf_op jit(solution)/shard_map/ppermute | solution.py:18
  124.9 5.3 collective-permute-start.3
  130.3 3.9 collective-permute-start.4
  131.6 6.5 %collective-permute-start.5 = (bf16[10,18,1,128]{3,1,2,0:T(8,128)(2,1)S(1)}, bf16[10,18,1,128]{3,1,2,0:T(8,128)(2,1)S(1)}, u32[]{:S(2)}, u32[]{:S(2)}) collective-permute-start(bf16[10,18,1,128]{3,1,2,0:T(8,128)(2,1)S(1)} %get-tuple-element.148), channel_id=1, source_target_pairs={{1,0},{3,2},{5,4},{7,6},{9,8},{11,10},{13,12},{15,14},{17,16},{19,... | collective-permute-start | bytes 138248 | tf_op jit(solution)/shard_map/ppermute | solution.py:21
  149.0 9.4 %copy-start.66 = (bf16[1024,128]{1,0:T(8,128)(2,1)}, bf16[1024,128]{1,0:T(8,128)(2,1)S(1)}, u32[]{:S(2)}) copy-start(bf16[1024,128]{1,0:T(8,128)(2,1)S(1)} %get-tuple-element.182) | copy-start | bytes 786436
  149.4 18.9 %collective-permute-start.6 = (bf16[1,16,8,128]{3,1,2,0:T(8,128)(2,1)S(1)}, bf16[1,16,8,128]{3,1,2,0:T(8,128)(2,1)S(1)}, u32[]{:S(2)}, u32[]{:S(2)}) collective-permute-start(bf16[1,16,8,128]{3,1,2,0:T(8,128)(2,1)S(1)} %get-tuple-element.176), channel_id=1, source_target_pairs={{0,16},{16,32},{32,48},{48,64},{64,80},{80,96},{96,112},{1,17},{17... | collective-permute-start | bytes 98312 | tf_op jit(solution)/shard_map/ppermute | solution.py:18
  153.1 15.3 %collective-permute-start.7 = (bf16[1,16,8,128]{3,1,2,0:T(8,128)(2,1)S(1)}, bf16[1,16,8,128]{3,1,2,0:T(8,128)(2,1)S(1)}, u32[]{:S(2)}, u32[]{:S(2)}) collective-permute-start(bf16[1,16,8,128]{3,1,2,0:T(8,128)(2,1)S(1)} %get-tuple-element.177), channel_id=1, source_target_pairs={{16,0},{32,16},{48,32},{64,48},{80,64},{96,80},{112,96},{17,1},{33... | collective-permute-start | bytes 98312 | tf_op jit(solution)/shard_map/ppermute | solution.py:21
  162.3 13.6 %copy-start.6 = (f32[27,128,128]{2,1,0:T(8,128)}, f32[27,128,128]{2,1,0:T(8,128)S(1)}, u32[]{:S(2)}) copy-start(f32[27,128,128]{2,1,0:T(8,128)S(1)} %fusion.32) | copy-start | bytes 5308420
  162.4 11.9 %collective-permute-start.18 = (bf16[1,16,8,128]{3,1,2,0:T(8,128)(2,1)S(1)}, bf16[1,16,8,128]{3,1,2,0:T(8,128)(2,1)S(1)}, u32[]{:S(2)}, u32[]{:S(2)}) collective-permute-start(bf16[1,16,8,128]{3,1,2,0:T(8,128)(2,1)S(1)} %get-tuple-element.168), channel_id=1, source_target_pairs={{0,16},{16,32},{32,48},{48,64},{64,80},{80,96},{96,112},{1,17},{17... | collective-permute-start | bytes 98312 | tf_op jit(solution)/shard_map/ppermute | solution.py:18
  167.1 7.2 %collective-permute-start.19 = (bf16[1,16,8,128]{3,1,2,0:T(8,128)(2,1)S(1)}, bf16[1,16,8,128]{3,1,2,0:T(8,128)(2,1)S(1)}, u32[]{:S(2)}, u32[]{:S(2)}) collective-permute-start(bf16[1,16,8,128]{3,1,2,0:T(8,128)(2,1)S(1)} %get-tuple-element.169), channel_id=1, source_target_pairs={{16,0},{32,16},{48,32},{64,48},{80,64},{96,80},{112,96},{17,1},{33... | collective-permute-start | bytes 98312 | tf_op jit(solution)/shard_map/ppermute | solution.py:21
  168.5 14.6 %collective-permute-start.8 = (bf16[10,1,8,128]{3,1,2,0:T(2,128)(2,1)S(1)}, bf16[10,1,8,128]{3,1,2,0:T(2,128)(2,1)S(1)}, u32[]{:S(2)}, u32[]{:S(2)}) collective-permute-start(bf16[10,1,8,128]{3,1,2,0:T(2,128)(2,1)S(1)} %get-tuple-element.160), channel_id=1, source_target_pairs={{0,2},{2,4},{4,6},{6,8},{8,10},{10,12},{12,14},{1,3},{3,5},{5,7},{... | collective-permute-start | bytes 61448 | tf_op jit(solution)/shard_map/ppermute | solution.py:18
  172.3 10.8 %collective-permute-start.9 = (bf16[10,1,8,128]{3,1,2,0:T(2,128)(2,1)S(1)}, bf16[10,1,8,128]{3,1,2,0:T(2,128)(2,1)S(1)}, u32[]{:S(2)}, u32[]{:S(2)}) collective-permute-start(bf16[10,1,8,128]{3,1,2,0:T(2,128)(2,1)S(1)} %get-tuple-element.161), channel_id=1, source_target_pairs={{2,0},{4,2},{6,4},{8,6},{10,8},{12,10},{14,12},{3,1},{5,3},{7,5},{... | collective-permute-start | bytes 61448 | tf_op jit(solution)/shard_map/ppermute | solution.py:21
  174.3 18.6 %copy-start.51 = (bf16[1,16,8,128]{3,1,2,0:T(8,128)(2,1)}, bf16[1,16,8,128]{3,1,2,0:T(8,128)(2,1)S(1)}, u32[]{:S(2)}) copy-start(bf16[1,16,8,128]{3,1,2,0:T(8,128)(2,1)S(1)} %collective-permute-done.19) | copy-start | bytes 98308
  176.8 14.8 %collective-permute-start.20 = (bf16[10,1,8,128]{3,1,2,0:T(2,128)(2,1)S(1)}, bf16[10,1,8,128]{3,1,2,0:T(2,128)(2,1)S(1)}, u32[]{:S(2)}, u32[]{:S(2)}) collective-permute-start(bf16[10,1,8,128]{3,1,2,0:T(2,128)(2,1)S(1)} %get-tuple-element.152), channel_id=1, source_target_pairs={{0,2},{2,4},{4,6},{6,8},{8,10},{10,12},{12,14},{1,3},{3,5},{5,7},{... | collective-permute-start | bytes 61448 | tf_op jit(solution)/shard_map/ppermute | solution.py:18
  180.4 11.2 %collective-permute-start.21 = (bf16[10,1,8,128]{3,1,2,0:T(2,128)(2,1)S(1)}, bf16[10,1,8,128]{3,1,2,0:T(2,128)(2,1)S(1)}, u32[]{:S(2)}, u32[]{:S(2)}) collective-permute-start(bf16[10,1,8,128]{3,1,2,0:T(2,128)(2,1)S(1)} %get-tuple-element.153), channel_id=1, source_target_pairs={{2,0},{4,2},{6,4},{8,6},{10,8},{12,10},{14,12},{3,1},{5,3},{7,5},{... | collective-permute-start | bytes 61448 | tf_op jit(solution)/shard_map/ppermute | solution.py:21
  183.2 22.8 %collective-permute-start.10 = (bf16[10,18,1,128]{3,1,2,0:T(8,128)(2,1)S(1)}, bf16[10,18,1,128]{3,1,2,0:T(8,128)(2,1)S(1)}, u32[]{:S(2)}, u32[]{:S(2)}) collective-permute-start(bf16[10,18,1,128]{3,1,2,0:T(8,128)(2,1)S(1)} %get-tuple-element.145), channel_id=1, source_target_pairs={{0,1},{2,3},{4,5},{6,7},{8,9},{10,11},{12,13},{14,15},{16,17},{18,... | collective-permute-start | bytes 138248 | tf_op jit(solution)/shard_map/ppermute | solution.py:18
  184.9 21.1 %collective-permute-start.11 = (bf16[10,18,1,128]{3,1,2,0:T(8,128)(2,1)S(1)}, bf16[10,18,1,128]{3,1,2,0:T(8,128)(2,1)S(1)}, u32[]{:S(2)}, u32[]{:S(2)}) collective-permute-start(bf16[10,18,1,128]{3,1,2,0:T(8,128)(2,1)S(1)} %get-tuple-element.144), channel_id=1, source_target_pairs={{1,0},{3,2},{5,4},{7,6},{9,8},{11,10},{13,12},{15,14},{17,16},{19,... | collective-permute-start | bytes 138248 | tf_op jit(solution)/shard_map/ppermute | solution.py:21
  193.7 59.3 %collective-permute-start.22 = (bf16[10,18,1,128]{3,1,2,0:T(8,128)(2,1)}, bf16[10,18,1,128]{3,1,2,0:T(8,128)(2,1)}, u32[]{:S(2)}, u32[]{:S(2)}) collective-permute-start(bf16[10,18,1,128]{3,1,2,0:T(8,128)(2,1)} %get-tuple-element.137), channel_id=1, source_target_pairs={{1,0},{3,2},{5,4},{7,6},{9,8},{11,10},{13,12},{15,14},{17,16},{19,... | collective-permute-start | bytes 138248 | tf_op jit(solution)/shard_map/ppermute | solution.py:21
  194.9 58.0 %collective-permute-start.23 = (bf16[10,18,1,128]{3,1,2,0:T(8,128)(2,1)}, bf16[10,18,1,128]{3,1,2,0:T(8,128)(2,1)}, u32[]{:S(2)}, u32[]{:S(2)}) collective-permute-start(bf16[10,18,1,128]{3,1,2,0:T(8,128)(2,1)} %get-tuple-element.136), channel_id=1, source_target_pairs={{0,1},{2,3},{4,5},{6,7},{8,9},{10,11},{12,13},{14,15},{16,17},{18,... | collective-permute-start | bytes 138248 | tf_op jit(solution)/shard_map/ppermute | solution.py:18
  235.7 8.0 %copy-start.12 = (bf16[8,16,8,128]{3,1,2,0:T(8,128)(2,1)S(1)}, bf16[8,16,8,128]{3,1,2,0:T(8,128)(2,1)}, u32[]{:S(2)}) copy-start(bf16[8,16,8,128]{3,1,2,0:T(8,128)(2,1)} %get-tuple-element.88) | copy-start | bytes 786436
  235.7 7.2 %copy-start.17 = (bf16[8,16,8,128]{3,1,2,0:T(8,128)(2,1)S(1)}, bf16[8,16,8,128]{3,1,2,0:T(8,128)(2,1)}, u32[]{:S(2)}) copy-start(bf16[8,16,8,128]{3,1,2,0:T(8,128)(2,1)} %get-tuple-element.80) | copy-start | bytes 786436
  235.7 8.7 %copy-start.16 = (bf16[8,16,8,128]{3,1,2,0:T(8,128)(2,1)S(1)}, bf16[8,16,8,128]{3,1,2,0:T(8,128)(2,1)}, u32[]{:S(2)}) copy-start(bf16[8,16,8,128]{3,1,2,0:T(8,128)(2,1)} %get-tuple-element.79) | copy-start | bytes 786436
  235.7 9.5 %copy-start.10 = (bf16[8,16,8,128]{3,1,2,0:T(8,128)(2,1)S(1)}, bf16[8,16,8,128]{3,1,2,0:T(8,128)(2,1)}, u32[]{:S(2)}) copy-start(bf16[8,16,8,128]{3,1,2,0:T(8,128)(2,1)} %get-tuple-element.87) | copy-start | bytes 786436
  237.5 8.4 %copy-start.15 = (bf16[8,16,8,128]{3,1,2,0:T(8,128)(2,1)S(1)}, bf16[8,16,8,128]{3,1,2,0:T(8,128)(2,1)}, u32[]{:S(2)}) copy-start(bf16[8,16,8,128]{3,1,2,0:T(8,128)(2,1)} %get-tuple-element.78) | copy-start | bytes 786436
  239.3 7.4 %copy-start.8 = (bf16[8,16,8,128]{3,1,2,0:T(8,128)(2,1)S(1)}, bf16[8,16,8,128]{3,1,2,0:T(8,128)(2,1)}, u32[]{:S(2)}) copy-start(bf16[8,16,8,128]{3,1,2,0:T(8,128)(2,1)} %get-tuple-element.86) | copy-start | bytes 786436
  241.1 6.4 %copy-start.14 = (bf16[8,16,8,128]{3,1,2,0:T(8,128)(2,1)S(1)}, bf16[8,16,8,128]{3,1,2,0:T(8,128)(2,1)}, u32[]{:S(2)}) copy-start(bf16[8,16,8,128]{3,1,2,0:T(8,128)(2,1)} %get-tuple-element.77) | copy-start | bytes 786436
  242.9 5.4 copy-start.7
  243.7 5.4 copy-start.13
  245.2 5.5 copy-start.11
  246.7 5.4 copy-start.9
  247.5 5.4 copy-start.52
  247.5 5.4 copy-start.62
  247.5 5.4 copy-start.64
  267.5 338.8 %all-reduce.5.cloned.1.call-start = ((), (), s32[]{:S(2)}) async-start(), calls=%async_computation.2 | async-start | bytes 7077888 | tf_op jit(solution)/shard_map/psum | solution.py:147
  606.2 3.1 copy-start.5
  (50 other events, 58.2 us)
Sparse Core Ops, SparseCore 0:
  267.6 162.4 all-reduce.6
  432.8 173.3 all-reduce.4
